TPU v7x, 512 devices: a whole 4x4x16 slice. The times are simulated.
512 devices in a mesh: test: 8 (over z_lo, core), bx: 4 (over y), by: 16 (over z_hi, x).
Axes of the slice: x: 4, y: 4, z: 16 (z_hi: 4, z_lo: 4; z = z_hi * 4 + z_lo), core: 2. Of those that a mesh axis runs over, the one named last changes fastest.
Arguments:
- log_conductivity: float32 [32, 128, 256], P('bx', 'by'), may hold values from -3 to 3
- storage: float32 [32, 128, 256], P('bx', 'by'), may hold values from 0.5 to 2
- recharge: float32 [32, 128, 256], P('bx', 'by'), may hold values from -6 to 6
- pump_rate: float32 [32], P('test'), may hold values from 4 to 16
- pump_well: int32 [32], P('test'), may hold values from 0 to 2047
- observed: float32 [32, 2048], P('test'), may hold values from -9 to 9
- owner: int32 [2048], replicated, may hold values from 0 to 63, as said below
- screen_column: int32 [2048], replicated, may hold values from 0 to 63
- screen_top: int32 [2048], replicated, may hold values from 0 to 248
Outputs:
- gradient: float32 [32, 128, 256], P('bx', 'by', 'test')
Inputs may be any that keep to these rules, and one draw needn't show every extreme that they name: `owner`: each brick owns exactly 32 wells.
All inputs are finite; a program needn't handle non-finite values.
Results may differ from a plain program's by a relative error of at most 0.0001.
Values sent between devices are 32-bit elements; how exact they have to be, the bound alone decides.
A program may use at most 64 MiB of HBM per device.

v0:
```python
import jax
import jax.numpy as jnp
from jax import lax
from jax.sharding import PartitionSpec as P

SWEEPS = 3
SCREEN = 8
epsilon = 1e-06


def with_halo(block, sides, width):
    for axis, dim in sides:
        count = lax.axis_size(axis)
        forward = [(i, i + 1) for i in range(count - 1)]
        backward = [(target, source) for source, target in forward]
        low = lax.ppermute(
            lax.slice_in_dim(block, block.shape[dim] - width, None, axis=dim), axis, forward
        )
        high = lax.ppermute(lax.slice_in_dim(block, 0, width, axis=dim), axis, backward)
        block = jnp.concatenate([low, block, high], axis=dim)
    return block


def pad_depth(values):
    return jnp.pad(values, [(0, 0)] * (values.ndim - 1) + [(1, 1)])


def neighbours(padded, centre):
    z_padded = pad_depth(centre)
    return [
        padded[..., 2:, 1:-1, :],
        padded[..., :-2, 1:-1, :],
        padded[..., 1:-1, 2:, :],
        padded[..., 1:-1, :-2, :],
        z_padded[..., 2:],
        z_padded[..., :-2],
    ]


def weighted(conductance, others):
    accumulated = conductance[0] * others[0]
    for position in range(1, 6):
        accumulated = accumulated + conductance[position] * others[position]
    return accumulated


def sensitivity(conductance, heads_field, heads_padded, adjoint_field, adjoint_padded):
    near_heads = neighbours(heads_padded, heads_field)
    near_adjoint = neighbours(adjoint_padded, adjoint_field)
    accumulated = jnp.zeros_like(heads_field)
    for position in range(6):
        accumulated = accumulated + conductance[position] * (heads_field - near_heads[position]) * (
            adjoint_field - near_adjoint[position]
        )
    return -0.5 * accumulated


def relax_field(source, conductance, diagonal):
    iterate = source / diagonal
    for sweep_index in range(SWEEPS - 1):
        padded = with_halo(iterate, (("bx", 1), ("by", 2)), 1)
        iterate = (source + weighted(conductance, neighbours(padded, iterate))) / diagonal
    return iterate


def per_sweep_terms(
    log_conductivity,
    storage,
    recharge,
    pump_rate,
    pump_well,
    observed,
    owner,
    screen_column,
    screen_top,
):
    size_x, size_y, size_z = log_conductivity.shape
    tests_here = pump_rate.shape[0]
    cell_count = size_x * size_y * size_z
    padded_log = with_halo(log_conductivity, (("bx", 0), ("by", 1)), 1)
    conductance = [
        jnp.exp(0.5 * (log_conductivity + other))
        for other in neighbours(padded_log, log_conductivity)
    ]
    diagonal = storage + weighted(conductance, [1.0] * 6)
    brick_index = lax.axis_index("bx") * lax.axis_size("by") + lax.axis_index("by")
    offsets = jnp.arange(SCREEN, dtype=jnp.int32)
    screen_cells = (screen_column * size_z + screen_top)[:, None] + offsets[None, :]
    owned_here = owner == brick_index
    pump_cells = screen_cells[pump_well]
    pump_value = jnp.where(owner[pump_well] == brick_index, -pump_rate, 0.0)
    test_rows = jnp.arange(tests_here, dtype=jnp.int32)[:, None]
    flat_source = jnp.broadcast_to(recharge.reshape(1, cell_count), (tests_here, cell_count))
    flat_source = flat_source.at[test_rows, pump_cells].add(
        jnp.broadcast_to(pump_value[:, None], pump_cells.shape)
    )
    source = flat_source.reshape(tests_here, size_x, size_y, size_z)
    heads_field = relax_field(source, conductance, diagonal)
    well_heads = jnp.mean(heads_field.reshape(tests_here, cell_count)[:, screen_cells], axis=2)
    residual = jnp.where(owned_here[None, :], well_heads - observed, 0.0)
    well_count = residual.shape[1]
    misfit = lax.psum(jnp.sum(residual * residual, axis=1), ("bx", "by")) / well_count + epsilon
    weights = residual / misfit[:, None]
    values = jnp.broadcast_to(weights[:, :, None], (tests_here, well_count, SCREEN)).reshape(
        tests_here, -1
    )
    adjoint_source = (
        jnp.zeros((tests_here, cell_count), jnp.float32).at[:, screen_cells.reshape(-1)].add(values)
    )
    adjoint_field = relax_field(
        adjoint_source.reshape(tests_here, size_x, size_y, size_z), conductance, diagonal
    )
    stacked = with_halo(
        jnp.concatenate([heads_field, adjoint_field], axis=0), (("bx", 1), ("by", 2)), 1
    )
    test_terms = sensitivity(
        conductance, heads_field, stacked[:tests_here], adjoint_field, stacked[tests_here:]
    )
    return (test_terms, misfit)


def local(
    log_conductivity,
    storage,
    recharge,
    pump_rate,
    pump_well,
    observed,
    owner,
    screen_column,
    screen_top,
):
    size_z = log_conductivity.shape[2]
    tests_here = pump_rate.shape[0]
    test_terms, misfit = per_sweep_terms(
        log_conductivity,
        storage,
        recharge,
        pump_rate,
        pump_well,
        observed,
        owner,
        screen_column,
        screen_top,
    )
    local_sum = jnp.sum(test_terms, axis=0)
    all_tests = tests_here * lax.axis_size("test")
    grand_total = lax.psum(local_sum, "test")
    slab_depth = size_z // lax.axis_size("test")
    gradient = lax.dynamic_slice_in_dim(
        grand_total, lax.axis_index("test") * slab_depth, slab_depth, 2
    )
    return gradient / all_tests


def solution(mesh):
    placed = (
        P("bx", "by", None),
        P("bx", "by", None),
        P("bx", "by", None),
        P("test"),
        P("test"),
        P("test", None),
        P(),
        P(),
        P(),
    )
    return jax.shard_map(
        local, mesh=mesh, in_specs=placed, out_specs=P("bx", "by", "test"), check_vma=False
    )
```

profile of v0, /device:TPU:2, one launch (start us, length us, event | category | flops | bytes accessed | tf_op | source)
XLA Modules:
  0.0 626.8 jit_solution(6473687219000279522)
XLA Ops:
  7.3 3.5 collective-permute-start.1
  16.6 5.6 collective-permute-start.2
  26.0 2.1 scatter_fusion
  30.8 5.2 collective-permute-start.5
  37.6 3.9 collective-permute-start.6
  44.3 3.1 collective-permute-done.7
  50.4 4.9 collective-permute-start.9
  58.8 4.6 collective-permute-start.11
  65.4 4.7 copy.20
  70.1 58.2 %gather_fusion.2 = f32[16384,4]{1,0:T(8,128)} fusion(f32[4,16384]{0,1:T(8,128)} %bitcast.34, s32[16384]{0:T(1024)S(1)} %broadcast_clamp_fusion), kind=kCustom, calls=%fused_computation.2 | custom fusion | bytes 589824 | tf_op jit(solution)/shard_map/gather | solution.py:99
  128.3 13.0 %bitcast_reduce_fusion = f32[2048,4]{1,0:T(8,128)S(1)} fusion(f32[16384,4]{1,0:T(8,128)} %gather_fusion.2), kind=kLoop, calls=%fused_computation.7 | loop fusion | flops 57344 | bytes 294912 | tf_op jit(solution)/shard_map/reduce_sum | solution.py:99
  142.5 236.4 %psum.14 = f32[4]{0:T(128)S(1)} all-reduce(f32[4]{0:T(128)S(1)} %multiply_reduce_fusion), channel_id=1, replica_groups=mesh['test'=8,'bx'=4,'by'=16] {'bx','by'}, use_global_device_ids=true, to_apply=%region_3.4 | all-reduce | flops 4 | bytes 32 | tf_op jit(solution)/shard_map/psum | solution.py:102
  379.4 91.6 %scatter_custom_fusion.1 = f32[4,16384]{0,1:T(8,128)} fusion(s32[16384]{0:T(1024)} %bitcast.41, f32[4,2048]{0,1:T(8,128)S(1)} %broadcast_divide_fusion, f32[]{:T(128)} %constant.27.clone.1), kind=kCustom, calls=%fused_computation.5 | custom fusion | flops 65536 | bytes 295424 | tf_op jit(solution)/shard_map/scatter-add | solution.py:108
  471.0 5.2 copy.24
  477.6 4.5 collective-permute-start.13
  483.8 4.0 collective-permute-start.14
  489.7 4.0 collective-permute-done.15
  495.2 4.9 collective-permute-start.17
  503.7 3.9 collective-permute-start.19
  507.6 1.9 collective-permute-done.19
  511.1 4.9 collective-permute-start.21
  519.9 3.9 collective-permute-start.23
  524.3 1.9 collective-permute-done.23
  527.4 91.2 %all-reduce.9.cloned.1.call-done = f32[8,8,256]{2,1,0:T(8,128)} async-done(((f32[8,8,256]{2,1,0:T(8,128)}), f32[8,8,256]{2,1,0:T(8,128)}) %all-reduce.9.cloned.1.call-update) | async-done | bytes 65552 | tf_op jit(solution)/shard_map/psum | solution.py:148
  (107 shorter events, 45.8 us)
Async XLA Ops:
  6.5 612.0 %all-reduce.9.cloned.1.call-start = ((), (), s32[]{:S(2)}) async-start(), calls=%async_computation | async-start | bytes 131072 | tf_op jit(solution)/shard_map/psum | solution.py:148
  7.3 8.4 %collective-permute-start.1 = (f32[1,8,256]{2,1,0:T(8,128)S(1)}, f32[1,8,256]{2,1,0:T(8,128)S(1)}, u32[]{:S(2)}, u32[]{:S(2)}) collective-permute-start(f32[1,8,256]{2,1,0:T(8,128)S(1)} %get-tuple-element.35), channel_id=1, source_target_pairs={{0,16},{16,32},{32,48},{1,17},{17,33},{33,49},{2,18},{18,34},{34,5... | collective-permute-start | bytes 24584 | tf_op jit(solution)/shard_map/ppermute | solution.py:16
  16.6 11.5 %collective-permute-start.2 = (f32[10,1,256]{2,1,0:T(1,128)S(1)}, f32[10,1,256]{2,1,0:T(1,128)S(1)}, u32[]{:S(2)}, u32[]{:S(2)}) collective-permute-start(f32[10,1,256]{2,1,0:T(1,128)S(1)} %get-tuple-element.33), channel_id=1, source_target_pairs={{1,0},{2,1},{3,2},{4,3},{5,4},{6,5},{7,6},{8,7},{9,8},{10,9},{11,1... | collective-permute-start | bytes 30728 | tf_op jit(solution)/shard_map/ppermute | solution.py:19
  22.2 5.9 collective-permute-start.3
  29.5 6.5 %collective-permute-start.4 = (f32[4,1,8,256]{3,2,1,0:T(8,128)S(1)}, f32[4,1,8,256]{3,2,1,0:T(8,128)S(1)}, u32[]{:S(2)}, u32[]{:S(2)}) collective-permute-start(f32[4,1,8,256]{3,2,1,0:T(8,128)S(1)} %get-tuple-element.31), channel_id=1, source_target_pairs={{16,0},{32,16},{48,32},{17,1},{33,17},{49,33},{18,2},{34,18},{50,3... | collective-permute-start | bytes 98312 | tf_op jit(solution)/shard_map/ppermute | solution.py:19
  30.8 6.8 %collective-permute-start.5 = (f32[4,1,8,256]{3,2,1,0:T(8,128)S(1)}, f32[4,1,8,256]{3,2,1,0:T(8,128)S(1)}, u32[]{:S(2)}, u32[]{:S(2)}) collective-permute-start(f32[4,1,8,256]{3,2,1,0:T(8,128)S(1)} %get-tuple-element.30), channel_id=1, source_target_pairs={{0,16},{16,32},{32,48},{1,17},{17,33},{33,49},{2,18},{18,34},{34,5... | collective-permute-start | bytes 98312 | tf_op jit(solution)/shard_map/ppermute | solution.py:16
  37.6 6.7 %collective-permute-start.6 = (f32[4,10,1,256]{3,2,1,0:T(1,128)S(1)}, f32[4,10,1,256]{3,2,1,0:T(1,128)S(1)}, u32[]{:S(2)}, u32[]{:S(2)}) collective-permute-start(f32[4,10,1,256]{3,2,1,0:T(1,128)S(1)} %get-tuple-element.22), channel_id=1, source_target_pairs={{1,0},{2,1},{3,2},{4,3},{5,4},{6,5},{7,6},{8,7},{9,8},{10,9},{11,1... | collective-permute-start | bytes 122888 | tf_op jit(solution)/shard_map/ppermute | solution.py:19
  41.5 5.9 collective-permute-start.7
  49.1 6.2 collective-permute-start.8
  50.4 6.4 %collective-permute-start.9 = (f32[4,1,8,256]{3,2,1,0:T(8,128)S(1)}, f32[4,1,8,256]{3,2,1,0:T(8,128)S(1)}, u32[]{:S(2)}, u32[]{:S(2)}) collective-permute-start(f32[4,1,8,256]{3,2,1,0:T(8,128)S(1)} %get-tuple-element.28), channel_id=1, source_target_pairs={{0,16},{16,32},{32,48},{1,17},{17,33},{33,49},{2,18},{18,34},{34,5... | collective-permute-start | bytes 98312 | tf_op jit(solution)/shard_map/ppermute | solution.py:16
  56.9 8.2 %collective-permute-start.10 = (f32[4,10,1,256]{3,2,1,0:T(1,128)S(1)}, f32[4,10,1,256]{3,2,1,0:T(1,128)S(1)}, u32[]{:S(2)}, u32[]{:S(2)}) collective-permute-start(f32[4,10,1,256]{3,2,1,0:T(1,128)S(1)} %get-tuple-element.20), channel_id=1, source_target_pairs={{1,0},{2,1},{3,2},{4,3},{5,4},{6,5},{7,6},{8,7},{9,8},{10,9},{11,1... | collective-permute-start | bytes 122888 | tf_op jit(solution)/shard_map/ppermute | solution.py:19
  58.8 6.3 %collective-permute-start.11 = (f32[4,10,1,256]{3,2,1,0:T(1,128)S(1)}, f32[4,10,1,256]{3,2,1,0:T(1,128)S(1)}, u32[]{:S(2)}, u32[]{:S(2)}) collective-permute-start(f32[4,10,1,256]{3,2,1,0:T(1,128)S(1)} %get-tuple-element.21), channel_id=1, source_target_pairs={{0,1},{1,2},{2,3},{3,4},{4,5},{5,6},{6,7},{7,8},{8,9},{9,10},{10,1... | collective-permute-start | bytes 122888 | tf_op jit(solution)/shard_map/ppermute | solution.py:16
  476.3 5.9 collective-permute-start.12
  477.6 6.1 collective-permute-start.13
  483.8 5.9 collective-permute-start.14
  487.8 5.9 collective-permute-start.15
  493.9 6.2 collective-permute-start.16
  495.2 6.4 %collective-permute-start.17 = (f32[4,1,8,256]{3,2,1,0:T(8,128)S(1)}, f32[4,1,8,256]{3,2,1,0:T(8,128)S(1)}, u32[]{:S(2)}, u32[]{:S(2)}) collective-permute-start(f32[4,1,8,256]{3,2,1,0:T(8,128)S(1)} %get-tuple-element.24), channel_id=1, source_target_pairs={{0,16},{16,32},{32,48},{1,17},{17,33},{33,49},{2,18},{18,34},{34,5... | collective-permute-start | bytes 98312 | tf_op jit(solution)/shard_map/ppermute | solution.py:16
  501.7 5.9 collective-permute-start.18
  503.7 5.9 collective-permute-start.19
  509.8 6.5 %collective-permute-start.20 = (f32[8,1,8,256]{3,2,1,0:T(8,128)S(1)}, f32[8,1,8,256]{3,2,1,0:T(8,128)S(1)}, u32[]{:S(2)}, u32[]{:S(2)}) collective-permute-start(f32[8,1,8,256]{3,2,1,0:T(8,128)S(1)} %get-tuple-element.15), channel_id=1, source_target_pairs={{16,0},{32,16},{48,32},{17,1},{33,17},{49,33},{18,2},{34,18},{50,3... | collective-permute-start | bytes 196616 | tf_op jit(solution)/shard_map/ppermute | solution.py:19
  511.1 6.7 %collective-permute-start.21 = (f32[8,1,8,256]{3,2,1,0:T(8,128)S(1)}, f32[8,1,8,256]{3,2,1,0:T(8,128)S(1)}, u32[]{:S(2)}, u32[]{:S(2)}) collective-permute-start(f32[8,1,8,256]{3,2,1,0:T(8,128)S(1)} %get-tuple-element.14), channel_id=1, source_target_pairs={{0,16},{16,32},{32,48},{1,17},{17,33},{33,49},{2,18},{18,34},{34,5... | collective-permute-start | bytes 196616 | tf_op jit(solution)/shard_map/ppermute | solution.py:16
  518.0 6.3 %collective-permute-start.22 = (f32[8,10,1,256]{3,2,1,0:T(1,128)S(1)}, f32[8,10,1,256]{3,2,1,0:T(1,128)S(1)}, u32[]{:S(2)}, u32[]{:S(2)}) collective-permute-start(f32[8,10,1,256]{3,2,1,0:T(1,128)S(1)} %get-tuple-element.12), channel_id=1, source_target_pairs={{1,0},{2,1},{3,2},{4,3},{5,4},{6,5},{7,6},{8,7},{9,8},{10,9},{11,1... | collective-permute-start | bytes 245768 | tf_op jit(solution)/shard_map/ppermute | solution.py:19
  519.9 6.3 %collective-permute-start.23 = (f32[8,10,1,256]{3,2,1,0:T(1,128)S(1)}, f32[8,10,1,256]{3,2,1,0:T(1,128)S(1)}, u32[]{:S(2)}, u32[]{:S(2)}) collective-permute-start(f32[8,10,1,256]{3,2,1,0:T(1,128)S(1)} %get-tuple-element.13), channel_id=1, source_target_pairs={{0,1},{1,2},{2,3},{3,4},{4,5},{5,6},{6,7},{7,8},{8,9},{9,10},{10,1... | collective-permute-start | bytes 245768 | tf_op jit(solution)/shard_map/ppermute | solution.py:16
  (14 other events, 841.6 us)
Sparse Core Ops, SparseCore 0:
  527.5 90.9 all-reduce.8
where the time goes:
time: 628 us; the launch traced here: 627 us
  blocking collectives  236 us (38%)
  other arithmetic  117 us (19%)
  waiting for transfers between devices  111 us (18%)
  local copies, waits for them, and re-layouts  75.6 us (12%)
  starting transfers between devices  73 us (12%)
  between operations  14 us (2%)
    psum x1, blocking collectives, per_sweep_terms(): lax.psum(jnp.sum(residual * residual, axis=1), ('bx', 'by')) / well_count  236 us
    scatter-add x1, other arithmetic, per_sweep_terms(): jnp.zeros((tests_here, cell_count), jnp.float32)  91.6 us
    psum x1, waiting for transfers between devices, local(): grand_total = lax.psum(local_sum, 'test')  91.2 us
    gather x1, local copies, waits for them, and re-layouts, per_sweep_terms(): heads_field.reshape(tests_here, cell_count)[:, screen_cells]  58.2 us
    ppermute x12, starting transfers between devices, with_halo(): lax.ppermute(lax.slice_in_dim(block, block.shape[dim] - width, None, axis...  45.9 us
    ppermute x12, starting transfers between devices, with_halo(): lax.ppermute(lax.slice_in_dim(block, 0, width, axis=dim), axis, backward)  27.1 us
    ppermute x12, waiting for transfers between devices, with_halo(): lax.ppermute(lax.slice_in_dim(block, block.shape[dim] - width, None, axis...  18.8 us
    reduce_sum x1, other arithmetic, per_sweep_terms(): jnp.mean(heads_field.reshape(tests_here, cell_count)[:, screen_cells], ax...  13 us
  transfers between devices with their start and end apart: 25, of which 12 were waited for; matrix products, arithmetic and copies ran while one was open for 2% of the time, Pallas kernels for 0%

commit v1 on v0

--- a/solution.py
+++ b/solution.py
@@ -99,7 +99,9 @@
     well_heads = jnp.mean(heads_field.reshape(tests_here, cell_count)[:, screen_cells], axis=2)
     residual = jnp.where(owned_here[None, :], well_heads - observed, 0.0)
     well_count = residual.shape[1]
-    misfit = lax.psum(jnp.sum(residual * residual, axis=1), ("bx", "by")) / well_count + epsilon
+    misfit = (
+        lax.psum(lax.psum(jnp.sum(residual * residual, axis=1), "bx"), "by") / well_count + epsilon
+    )
     weights = residual / misfit[:, None]
     values = jnp.broadcast_to(weights[:, :, None], (tests_here, well_count, SCREEN)).reshape(
         tests_here, -1

time: 628 us -> 483 us (0.77)
  blocking collectives: 236 us -> 78.2 us
  waiting for transfers between devices: 111 us -> 123 us
    psum x1 -> x2, blocking collectives: 236 us -> 78.2 us  [the longest x1 65.6 us: per_sweep_terms(): lax.psum(lax.psum(jnp.sum(residual * residual, axis=1), 'bx'), 'by')]
    psum x1, waiting for transfers between devices: 91.2 us -> 103 us  [local(): grand_total = lax.psum(local_sum, 'test')]
  transfers between devices with their start and end apart: 25 -> 25, of which waited for: 12 -> 13; matrix products, arithmetic and copies ran while one was open for 2% -> 2% of each run, Pallas kernels for 0% -> 0%
where the time goes in v1:
time: 483 us; the launch traced here: 482 us
  waiting for transfers between devices  123 us (25%)
  other arithmetic  118 us (24%)
  blocking collectives  78.2 us (16%)
  local copies, waits for them, and re-layouts  74.9 us (16%)
  starting transfers between devices  72.9 us (15%)
  between operations  14 us (3%)
    psum x1, waiting for transfers between devices, local(): grand_total = lax.psum(local_sum, 'test')  103 us
    scatter-add x1, other arithmetic, per_sweep_terms(): jnp.zeros((tests_here, cell_count), jnp.float32)  91.6 us
    psum x1, blocking collectives, per_sweep_terms(): lax.psum(lax.psum(jnp.sum(residual * residual, axis=1), 'bx'), 'by')  65.6 us
    gather x1, local copies, waits for them, and re-layouts, per_sweep_terms(): heads_field.reshape(tests_here, cell_count)[:, screen_cells]  58.1 us
    ppermute x12, starting transfers between devices, with_halo(): lax.ppermute(lax.slice_in_dim(block, block.shape[dim] - width, None, axis...  45.9 us
    ppermute x12, starting transfers between devices, with_halo(): lax.ppermute(lax.slice_in_dim(block, 0, width, axis=dim), axis, backward)  27 us
    ppermute x12, waiting for transfers between devices, with_halo(): lax.ppermute(lax.slice_in_dim(block, block.shape[dim] - width, None, axis...  19.9 us
    reduce_sum x1, other arithmetic, per_sweep_terms(): jnp.mean(heads_field.reshape(tests_here, cell_count)[:, screen_cells], ax...  13 us
  transfers between devices with their start and end apart: 25, of which 13 were waited for; matrix products, arithmetic and copies ran while one was open for 2% of the time, Pallas kernels for 0%

profile of v1, /device:TPU:2, one launch (start us, length us, event | category | flops | bytes accessed | tf_op | source)
XLA Modules:
  0.0 481.6 jit_solution(11520950937153014484)
XLA Ops:
  7.3 3.5 collective-permute-start.1
  16.6 5.6 %collective-permute-start.2 = (f32[10,1,256]{2,1,0:T(1,128)S(1)}, f32[10,1,256]{2,1,0:T(1,128)S(1)}, u32[]{:S(2)}, u32[]{:S(2)}) collective-permute-start(f32[10,1,256]{2,1,0:T(1,128)S(1)} %get-tuple-element.33), channel_id=1, source_target_pairs={{1,0},{2,1},{3,2},{4,3},{5,4},{6,5},{7,6},{8,7},{9,8},{10,9},{11,1... | collective-permute-start | bytes 30728 | tf_op jit(solution)/shard_map/ppermute | solution.py:19
  26.0 2.1 scatter_fusion
  30.8 5.2 %collective-permute-start.5 = (f32[4,1,8,256]{3,2,1,0:T(8,128)S(1)}, f32[4,1,8,256]{3,2,1,0:T(8,128)S(1)}, u32[]{:S(2)}, u32[]{:S(2)}) collective-permute-start(f32[4,1,8,256]{3,2,1,0:T(8,128)S(1)} %get-tuple-element.30), channel_id=1, source_target_pairs={{0,16},{16,32},{32,48},{1,17},{17,33},{33,49},{2,18},{18,34},{34,5... | collective-permute-start | bytes 98312 | tf_op jit(solution)/shard_map/ppermute | solution.py:16
  37.6 3.9 collective-permute-start.6
  44.3 3.1 collective-permute-done.7
  49.0 4.9 %collective-permute-start.9 = (f32[4,1,8,256]{3,2,1,0:T(8,128)S(1)}, f32[4,1,8,256]{3,2,1,0:T(8,128)S(1)}, u32[]{:S(2)}, u32[]{:S(2)}) collective-permute-start(f32[4,1,8,256]{3,2,1,0:T(8,128)S(1)} %get-tuple-element.28), channel_id=1, source_target_pairs={{0,16},{16,32},{32,48},{1,17},{17,33},{33,49},{2,18},{18,34},{34,5... | collective-permute-start | bytes 98312 | tf_op jit(solution)/shard_map/ppermute | solution.py:16
  57.4 4.6 collective-permute-start.11
  64.9 4.7 copy.20
  69.7 58.1 %gather_fusion.2 = f32[16384,4]{1,0:T(8,128)} fusion(f32[4,16384]{0,1:T(8,128)} %bitcast.34, s32[16384]{0:T(1024)S(1)} %broadcast_clamp_fusion), kind=kCustom, calls=%fused_computation.2 | custom fusion | bytes 589824 | tf_op jit(solution)/shard_map/gather | solution.py:99
  127.8 13.0 %bitcast_reduce_fusion = f32[2048,4]{1,0:T(8,128)S(1)} fusion(f32[16384,4]{1,0:T(8,128)} %gather_fusion.2), kind=kLoop, calls=%fused_computation.7 | loop fusion | flops 57344 | bytes 294912 | tf_op jit(solution)/shard_map/reduce_sum | solution.py:99
  142.4 12.6 %psum.21 = f32[4]{0:T(128)S(1)} all-reduce(f32[4]{0:T(128)S(1)} %multiply_reduce_fusion), channel_id=1, replica_groups=mesh['test'=8,'bx'=4,'by'=16] {'bx'}, use_global_device_ids=true, to_apply=%region_3.4 | all-reduce | flops 4 | bytes 32 | tf_op jit(solution)/shard_map/psum | solution.py:103
  156.6 65.6 %psum.22 = f32[4]{0:T(128)S(1)} all-reduce(f32[4]{0:T(128)S(1)} %psum.21), channel_id=1, replica_groups=mesh['test'=8,'bx'=4,'by'=16] {'by'}, use_global_device_ids=true, to_apply=%region_4.5 | all-reduce | flops 4 | bytes 32 | tf_op jit(solution)/shard_map/psum | solution.py:103
  222.7 91.6 %scatter_custom_fusion.1 = f32[4,16384]{0,1:T(8,128)} fusion(s32[16384]{0:T(1024)} %bitcast.41, f32[4,2048]{0,1:T(8,128)S(1)} %broadcast_divide_fusion, f32[]{:T(128)} %constant.27.clone.1), kind=kCustom, calls=%fused_computation.5 | custom fusion | flops 65536 | bytes 295424 | tf_op jit(solution)/shard_map/scatter-add | solution.py:110
  314.2 5.2 %copy.24 = f32[4,8,8,256]{3,2,1,0:T(8,128)S(1)} copy(f32[4,8,8,256]{0,3,2,1:T(8,128)} %bitcast.38) | data formatting | bytes 524288 | tf_op jit(solution)/shard_map/reshape | solution.py:113
  320.8 4.5 collective-permute-start.13
  327.0 3.9 collective-permute-start.14
  332.9 3.9 collective-permute-done.15
  338.4 4.9 %collective-permute-start.17 = (f32[4,1,8,256]{3,2,1,0:T(8,128)S(1)}, f32[4,1,8,256]{3,2,1,0:T(8,128)S(1)}, u32[]{:S(2)}, u32[]{:S(2)}) collective-permute-start(f32[4,1,8,256]{3,2,1,0:T(8,128)S(1)} %get-tuple-element.24), channel_id=1, source_target_pairs={{0,16},{16,32},{32,48},{1,17},{17,33},{33,49},{2,18},{18,34},{34,5... | collective-permute-start | bytes 98312 | tf_op jit(solution)/shard_map/ppermute | solution.py:16
  346.9 3.9 collective-permute-start.19
  350.8 1.9 collective-permute-done.19
  354.3 4.9 %collective-permute-start.21 = (f32[8,1,8,256]{3,2,1,0:T(8,128)S(1)}, f32[8,1,8,256]{3,2,1,0:T(8,128)S(1)}, u32[]{:S(2)}, u32[]{:S(2)}) collective-permute-start(f32[8,1,8,256]{3,2,1,0:T(8,128)S(1)} %get-tuple-element.14), channel_id=1, source_target_pairs={{0,16},{16,32},{32,48},{1,17},{17,33},{33,49},{2,18},{18,34},{34,5... | collective-permute-start | bytes 196616 | tf_op jit(solution)/shard_map/ppermute | solution.py:16
  363.1 3.9 collective-permute-start.23
  370.6 102.7 %all-reduce.9.cloned.1.call-done = f32[8,8,256]{2,1,0:T(8,128)} async-done(((f32[8,8,256]{2,1,0:T(8,128)}), f32[8,8,256]{2,1,0:T(8,128)}) %all-reduce.9.cloned.1.call-update) | async-done | bytes 65552 | tf_op jit(solution)/shard_map/psum | solution.py:150
  (106 shorter events, 49.2 us)
Async XLA Ops:
  6.5 466.7 %all-reduce.9.cloned.1.call-start = ((), (), s32[]{:S(2)}) async-start(), calls=%async_computation | async-start | bytes 131072 | tf_op jit(solution)/shard_map/psum | solution.py:150
  7.3 8.4 %collective-permute-start.1 = (f32[1,8,256]{2,1,0:T(8,128)S(1)}, f32[1,8,256]{2,1,0:T(8,128)S(1)}, u32[]{:S(2)}, u32[]{:S(2)}) collective-permute-start(f32[1,8,256]{2,1,0:T(8,128)S(1)} %get-tuple-element.35), channel_id=1, source_target_pairs={{0,16},{16,32},{32,48},{1,17},{17,33},{33,49},{2,18},{18,34},{34,5... | collective-permute-start | bytes 24584 | tf_op jit(solution)/shard_map/ppermute | solution.py:16
  16.6 11.5 %collective-permute-start.2 = (f32[10,1,256]{2,1,0:T(1,128)S(1)}, f32[10,1,256]{2,1,0:T(1,128)S(1)}, u32[]{:S(2)}, u32[]{:S(2)}) collective-permute-start(f32[10,1,256]{2,1,0:T(1,128)S(1)} %get-tuple-element.33), channel_id=1, source_target_pairs={{1,0},{2,1},{3,2},{4,3},{5,4},{6,5},{7,6},{8,7},{9,8},{10,9},{11,1... | collective-permute-start | bytes 30728 | tf_op jit(solution)/shard_map/ppermute | solution.py:19
  22.2 5.9 %collective-permute-start.3 = (f32[10,1,256]{2,1,0:T(1,128)S(1)}, f32[10,1,256]{2,1,0:T(1,128)S(1)}, u32[]{:S(2)}, u32[]{:S(2)}) collective-permute-start(f32[10,1,256]{2,1,0:T(1,128)S(1)} %get-tuple-element.32), channel_id=1, source_target_pairs={{0,1},{1,2},{2,3},{3,4},{4,5},{5,6},{6,7},{7,8},{8,9},{9,10},{10,1... | collective-permute-start | bytes 30728 | tf_op jit(solution)/shard_map/ppermute | solution.py:16
  29.5 6.5 %collective-permute-start.4 = (f32[4,1,8,256]{3,2,1,0:T(8,128)S(1)}, f32[4,1,8,256]{3,2,1,0:T(8,128)S(1)}, u32[]{:S(2)}, u32[]{:S(2)}) collective-permute-start(f32[4,1,8,256]{3,2,1,0:T(8,128)S(1)} %get-tuple-element.31), channel_id=1, source_target_pairs={{16,0},{32,16},{48,32},{17,1},{33,17},{49,33},{18,2},{34,18},{50,3... | collective-permute-start | bytes 98312 | tf_op jit(solution)/shard_map/ppermute | solution.py:19
  30.8 6.8 %collective-permute-start.5 = (f32[4,1,8,256]{3,2,1,0:T(8,128)S(1)}, f32[4,1,8,256]{3,2,1,0:T(8,128)S(1)}, u32[]{:S(2)}, u32[]{:S(2)}) collective-permute-start(f32[4,1,8,256]{3,2,1,0:T(8,128)S(1)} %get-tuple-element.30), channel_id=1, source_target_pairs={{0,16},{16,32},{32,48},{1,17},{17,33},{33,49},{2,18},{18,34},{34,5... | collective-permute-start | bytes 98312 | tf_op jit(solution)/shard_map/ppermute | solution.py:16
  37.6 6.7 %collective-permute-start.6 = (f32[4,10,1,256]{3,2,1,0:T(1,128)S(1)}, f32[4,10,1,256]{3,2,1,0:T(1,128)S(1)}, u32[]{:S(2)}, u32[]{:S(2)}) collective-permute-start(f32[4,10,1,256]{3,2,1,0:T(1,128)S(1)} %get-tuple-element.22), channel_id=1, source_target_pairs={{1,0},{2,1},{3,2},{4,3},{5,4},{6,5},{7,6},{8,7},{9,8},{10,9},{11,1... | collective-permute-start | bytes 122888 | tf_op jit(solution)/shard_map/ppermute | solution.py:19
  41.5 5.9 %collective-permute-start.7 = (f32[4,10,1,256]{3,2,1,0:T(1,128)S(1)}, f32[4,10,1,256]{3,2,1,0:T(1,128)S(1)}, u32[]{:S(2)}, u32[]{:S(2)}) collective-permute-start(f32[4,10,1,256]{3,2,1,0:T(1,128)S(1)} %get-tuple-element.23), channel_id=1, source_target_pairs={{0,1},{1,2},{2,3},{3,4},{4,5},{5,6},{6,7},{7,8},{8,9},{9,10},{10,1... | collective-permute-start | bytes 122888 | tf_op jit(solution)/shard_map/ppermute | solution.py:16
  47.7 6.2 %collective-permute-start.8 = (f32[4,1,8,256]{3,2,1,0:T(8,128)S(1)}, f32[4,1,8,256]{3,2,1,0:T(8,128)S(1)}, u32[]{:S(2)}, u32[]{:S(2)}) collective-permute-start(f32[4,1,8,256]{3,2,1,0:T(8,128)S(1)} %get-tuple-element.29), channel_id=1, source_target_pairs={{16,0},{32,16},{48,32},{17,1},{33,17},{49,33},{18,2},{34,18},{50,3... | collective-permute-start | bytes 98312 | tf_op jit(solution)/shard_map/ppermute | solution.py:19
  49.0 6.4 %collective-permute-start.9 = (f32[4,1,8,256]{3,2,1,0:T(8,128)S(1)}, f32[4,1,8,256]{3,2,1,0:T(8,128)S(1)}, u32[]{:S(2)}, u32[]{:S(2)}) collective-permute-start(f32[4,1,8,256]{3,2,1,0:T(8,128)S(1)} %get-tuple-element.28), channel_id=1, source_target_pairs={{0,16},{16,32},{32,48},{1,17},{17,33},{33,49},{2,18},{18,34},{34,5... | collective-permute-start | bytes 98312 | tf_op jit(solution)/shard_map/ppermute | solution.py:16
  55.5 7.0 %collective-permute-start.10 = (f32[4,10,1,256]{3,2,1,0:T(1,128)S(1)}, f32[4,10,1,256]{3,2,1,0:T(1,128)S(1)}, u32[]{:S(2)}, u32[]{:S(2)}) collective-permute-start(f32[4,10,1,256]{3,2,1,0:T(1,128)S(1)} %get-tuple-element.20), channel_id=1, source_target_pairs={{1,0},{2,1},{3,2},{4,3},{5,4},{6,5},{7,6},{8,7},{9,8},{10,9},{11,1... | collective-permute-start | bytes 122888 | tf_op jit(solution)/shard_map/ppermute | solution.py:19
  57.4 6.2 %collective-permute-start.11 = (f32[4,10,1,256]{3,2,1,0:T(1,128)S(1)}, f32[4,10,1,256]{3,2,1,0:T(1,128)S(1)}, u32[]{:S(2)}, u32[]{:S(2)}) collective-permute-start(f32[4,10,1,256]{3,2,1,0:T(1,128)S(1)} %get-tuple-element.21), channel_id=1, source_target_pairs={{0,1},{1,2},{2,3},{3,4},{4,5},{5,6},{6,7},{7,8},{8,9},{9,10},{10,1... | collective-permute-start | bytes 122888 | tf_op jit(solution)/shard_map/ppermute | solution.py:16
  319.5 5.9 %collective-permute-start.12 = (f32[4,1,8,256]{3,2,1,0:T(8,128)S(1)}, f32[4,1,8,256]{3,2,1,0:T(8,128)S(1)}, u32[]{:S(2)}, u32[]{:S(2)}) collective-permute-start(f32[4,1,8,256]{3,2,1,0:T(8,128)S(1)} %get-tuple-element.27), channel_id=1, source_target_pairs={{16,0},{32,16},{48,32},{17,1},{33,17},{49,33},{18,2},{34,18},{50,3... | collective-permute-start | bytes 98312 | tf_op jit(solution)/shard_map/ppermute | solution.py:19
  320.8 6.1 %collective-permute-start.13 = (f32[4,1,8,256]{3,2,1,0:T(8,128)S(1)}, f32[4,1,8,256]{3,2,1,0:T(8,128)S(1)}, u32[]{:S(2)}, u32[]{:S(2)}) collective-permute-start(f32[4,1,8,256]{3,2,1,0:T(8,128)S(1)} %get-tuple-element.26), channel_id=1, source_target_pairs={{0,16},{16,32},{32,48},{1,17},{17,33},{33,49},{2,18},{18,34},{34,5... | collective-permute-start | bytes 98312 | tf_op jit(solution)/shard_map/ppermute | solution.py:16
  327.0 5.9 %collective-permute-start.14 = (f32[4,10,1,256]{3,2,1,0:T(1,128)S(1)}, f32[4,10,1,256]{3,2,1,0:T(1,128)S(1)}, u32[]{:S(2)}, u32[]{:S(2)}) collective-permute-start(f32[4,10,1,256]{3,2,1,0:T(1,128)S(1)} %get-tuple-element.18), channel_id=1, source_target_pairs={{1,0},{2,1},{3,2},{4,3},{5,4},{6,5},{7,6},{8,7},{9,8},{10,9},{11,1... | collective-permute-start | bytes 122888 | tf_op jit(solution)/shard_map/ppermute | solution.py:19
  330.9 5.9 %collective-permute-start.15 = (f32[4,10,1,256]{3,2,1,0:T(1,128)S(1)}, f32[4,10,1,256]{3,2,1,0:T(1,128)S(1)}, u32[]{:S(2)}, u32[]{:S(2)}) collective-permute-start(f32[4,10,1,256]{3,2,1,0:T(1,128)S(1)} %get-tuple-element.19), channel_id=1, source_target_pairs={{0,1},{1,2},{2,3},{3,4},{4,5},{5,6},{6,7},{7,8},{8,9},{9,10},{10,1... | collective-permute-start | bytes 122888 | tf_op jit(solution)/shard_map/ppermute | solution.py:16
  337.1 6.2 %collective-permute-start.16 = (f32[4,1,8,256]{3,2,1,0:T(8,128)S(1)}, f32[4,1,8,256]{3,2,1,0:T(8,128)S(1)}, u32[]{:S(2)}, u32[]{:S(2)}) collective-permute-start(f32[4,1,8,256]{3,2,1,0:T(8,128)S(1)} %get-tuple-element.25), channel_id=1, source_target_pairs={{16,0},{32,16},{48,32},{17,1},{33,17},{49,33},{18,2},{34,18},{50,3... | collective-permute-start | bytes 98312 | tf_op jit(solution)/shard_map/ppermute | solution.py:19
  338.4 6.4 %collective-permute-start.17 = (f32[4,1,8,256]{3,2,1,0:T(8,128)S(1)}, f32[4,1,8,256]{3,2,1,0:T(8,128)S(1)}, u32[]{:S(2)}, u32[]{:S(2)}) collective-permute-start(f32[4,1,8,256]{3,2,1,0:T(8,128)S(1)} %get-tuple-element.24), channel_id=1, source_target_pairs={{0,16},{16,32},{32,48},{1,17},{17,33},{33,49},{2,18},{18,34},{34,5... | collective-permute-start | bytes 98312 | tf_op jit(solution)/shard_map/ppermute | solution.py:16
  344.9 5.9 %collective-permute-start.18 = (f32[4,10,1,256]{3,2,1,0:T(1,128)S(1)}, f32[4,10,1,256]{3,2,1,0:T(1,128)S(1)}, u32[]{:S(2)}, u32[]{:S(2)}) collective-permute-start(f32[4,10,1,256]{3,2,1,0:T(1,128)S(1)} %get-tuple-element.16), channel_id=1, source_target_pairs={{1,0},{2,1},{3,2},{4,3},{5,4},{6,5},{7,6},{8,7},{9,8},{10,9},{11,1... | collective-permute-start | bytes 122888 | tf_op jit(solution)/shard_map/ppermute | solution.py:19
  346.9 5.9 %collective-permute-start.19 = (f32[4,10,1,256]{3,2,1,0:T(1,128)S(1)}, f32[4,10,1,256]{3,2,1,0:T(1,128)S(1)}, u32[]{:S(2)}, u32[]{:S(2)}) collective-permute-start(f32[4,10,1,256]{3,2,1,0:T(1,128)S(1)} %get-tuple-element.17), channel_id=1, source_target_pairs={{0,1},{1,2},{2,3},{3,4},{4,5},{5,6},{6,7},{7,8},{8,9},{9,10},{10,1... | collective-permute-start | bytes 122888 | tf_op jit(solution)/shard_map/ppermute | solution.py:16
  353.0 6.5 %collective-permute-start.20 = (f32[8,1,8,256]{3,2,1,0:T(8,128)S(1)}, f32[8,1,8,256]{3,2,1,0:T(8,128)S(1)}, u32[]{:S(2)}, u32[]{:S(2)}) collective-permute-start(f32[8,1,8,256]{3,2,1,0:T(8,128)S(1)} %get-tuple-element.15), channel_id=1, source_target_pairs={{16,0},{32,16},{48,32},{17,1},{33,17},{49,33},{18,2},{34,18},{50,3... | collective-permute-start | bytes 196616 | tf_op jit(solution)/shard_map/ppermute | solution.py:19
  354.3 6.7 %collective-permute-start.21 = (f32[8,1,8,256]{3,2,1,0:T(8,128)S(1)}, f32[8,1,8,256]{3,2,1,0:T(8,128)S(1)}, u32[]{:S(2)}, u32[]{:S(2)}) collective-permute-start(f32[8,1,8,256]{3,2,1,0:T(8,128)S(1)} %get-tuple-element.14), channel_id=1, source_target_pairs={{0,16},{16,32},{32,48},{1,17},{17,33},{33,49},{2,18},{18,34},{34,5... | collective-permute-start | bytes 196616 | tf_op jit(solution)/shard_map/ppermute | solution.py:16
  361.2 6.3 %collective-permute-start.22 = (f32[8,10,1,256]{3,2,1,0:T(1,128)S(1)}, f32[8,10,1,256]{3,2,1,0:T(1,128)S(1)}, u32[]{:S(2)}, u32[]{:S(2)}) collective-permute-start(f32[8,10,1,256]{3,2,1,0:T(1,128)S(1)} %get-tuple-element.12), channel_id=1, source_target_pairs={{1,0},{2,1},{3,2},{4,3},{5,4},{6,5},{7,6},{8,7},{9,8},{10,9},{11,1... | collective-permute-start | bytes 245768 | tf_op jit(solution)/shard_map/ppermute | solution.py:19
  363.1 6.3 %collective-permute-start.23 = (f32[8,10,1,256]{3,2,1,0:T(1,128)S(1)}, f32[8,10,1,256]{3,2,1,0:T(1,128)S(1)}, u32[]{:S(2)}, u32[]{:S(2)}) collective-permute-start(f32[8,10,1,256]{3,2,1,0:T(1,128)S(1)} %get-tuple-element.13), channel_id=1, source_target_pairs={{0,1},{1,2},{2,3},{3,4},{4,5},{5,6},{6,7},{7,8},{8,9},{9,10},{10,1... | collective-permute-start | bytes 245768 | tf_op jit(solution)/shard_map/ppermute | solution.py:16
  (13 other events, 851.4 us)
Sparse Core Ops, SparseCore 0:
  370.7 102.5 all-reduce.8
